TPU v7x, 32 devices: a whole 2x2x4 slice. The times are simulated.
32 devices in a mesh: section: 4 (over y, x), feat: 4 (over z), dp: 2 (over core).
Axes of the slice: x: 2, y: 2, z: 4, core: 2. Of those that a mesh axis runs over, the one named last changes fastest.
Arguments:
- section_outputs: bfloat16 [4, 1024, 4608], P('section', 'dp', 'feat'), may hold values from -6 to 6
- enc_weight: bfloat16 [4608, 16384], P('dp', ('section', 'feat')), may hold values from -0.09375 to 0.09375
- enc_bias: float32 [16384], P(('section', 'feat')), may hold values from -3 to 3
- thresholds: int32 [16384], P(('section', 'feat')), may hold values from 0 to 7
- dec_weight: bfloat16 [16384, 4608], P(('section', 'feat'), 'dp'), may hold values from -0.09375 to 0.09375
- dec_bias: float32 [4608], replicated, may hold values from -3 to 3
- enc_moment: float32 [4608, 16384], P('dp', ('section', 'feat')), may hold values from -2 to 2
- enc_second: float32 [4608, 16384], P('dp', ('section', 'feat')), may hold values from 0.01 to 1
- dec_moment: float32 [16384, 4608], P(('section', 'feat'), 'dp'), may hold values from -2 to 2
- dec_second: float32 [16384, 4608], P(('section', 'feat'), 'dp'), may hold values from 0.01 to 1
Outputs:
- enc_update: bfloat16 [4608, 16384], P('dp', ('section', 'feat'))
- enc_moment_new: float32 [4608, 16384], P('dp', ('section', 'feat'))
- enc_second_new: float32 [4608, 16384], P('dp', ('section', 'feat'))
- dec_update: bfloat16 [16384, 4608], P(('section', 'feat'), 'dp')
- dec_moment_new: float32 [16384, 4608], P(('section', 'feat'), 'dp')
- dec_second_new: float32 [16384, 4608], P(('section', 'feat'), 'dp')
All inputs are finite; a program needn't handle non-finite values.
Results may differ from a plain program's by a relative error of at most 0.0055.
The roundings to bfloat16 on the way count: a program that leaves them out, or rounds other values in their place, can miss the bound.
Values may be sent and summed in bfloat16 or wider, within the bound.
No kernel may reach another device: no remote copies, remote signals or barrier semaphores. Data moves between devices by JAX's collectives and lax.ppermute only.
A program may use at most 256 MiB of HBM per device.

v0:
```python
import math
import jax
import jax.numpy as jnp
from jax import lax
from jax.sharding import PartitionSpec as P

band = 0.1
level_step = 0.25
beta_first = 0.9
beta_second = 0.999
fix_first = 1.0 - (0.9**50) ** 2
fix_second = 1.0 - (0.999**50) ** 2
epsilon = 1e-08


def adam_moves(moment, second, grads):
    moment_new = beta_first * moment + (1.0 - beta_first) * grads
    second_new = beta_second * second + (1.0 - beta_second) * grads * grads
    update = (moment_new / fix_first / (jnp.sqrt(second_new / fix_second) + epsilon)).astype(
        jnp.bfloat16
    )
    return (update, moment_new, second_new)


def on_device(
    section_outputs,
    enc_weight,
    enc_bias,
    thresholds,
    dec_weight,
    dec_bias,
    enc_moment,
    enc_second,
    dec_moment,
    dec_second,
):
    own_part = section_outputs[0].astype(jnp.float32)
    summed = lax.psum(own_part, "section").astype(jnp.bfloat16)
    resid = lax.all_gather(summed, "feat", axis=1, tiled=True)
    tok_rows = resid.shape[0]
    token_total = tok_rows * lax.axis_size("dp")
    columns = resid
    preact = (
        jnp.dot(
            columns,
            lax.all_gather(enc_weight, "dp", axis=0, tiled=True),
            preferred_element_type=jnp.float32,
        )
        + enc_bias
    )
    theta = level_step * (thresholds.astype(jnp.float32) + 1.0)
    opened = jax.nn.sigmoid((preact - theta) / band)
    codes = (preact * opened).astype(jnp.bfloat16)
    dec_full = lax.all_gather(dec_weight, "dp", axis=1, tiled=True)
    groups = lax.axis_size(("section", "feat"))
    position = lax.axis_index(("section", "feat"))
    span = tok_rows // groups
    recon = lax.psum_scatter(
        jnp.dot(codes, dec_full, preferred_element_type=jnp.float32),
        ("section", "feat"),
        scatter_dimension=0,
        tiled=True,
    )
    first = position * span
    target = lax.dynamic_slice_in_dim(resid, first, span, 0).astype(jnp.float32)
    error_part = ((recon + dec_bias - target) / math.sqrt(token_total)).astype(jnp.bfloat16)
    grad_out = lax.all_gather(error_part, ("section", "feat"), axis=0, tiled=True)
    dec_whole = lax.dot_general(
        codes, grad_out, (((0,), (0,)), ((), ())), preferred_element_type=jnp.float32
    )
    dec_grad = lax.psum_scatter(dec_whole, "dp", scatter_dimension=1, tiled=True)
    back = lax.dot_general(
        grad_out, dec_full, (((1,), (1,)), ((), ())), preferred_element_type=jnp.float32
    )
    pre_grad = (back * (opened + preact * opened * (1.0 - opened) / band)).astype(jnp.bfloat16)
    columns = resid
    enc_grad = lax.psum_scatter(
        lax.dot_general(
            columns, pre_grad, (((0,), (0,)), ((), ())), preferred_element_type=jnp.float32
        ),
        "dp",
        scatter_dimension=0,
        tiled=True,
    )
    enc_update, enc_moment_new, enc_second_new = adam_moves(enc_moment, enc_second, enc_grad)
    dec_update, dec_moment_new, dec_second_new = adam_moves(dec_moment, dec_second, dec_grad)
    return (enc_update, enc_moment_new, enc_second_new, dec_update, dec_moment_new, dec_second_new)


def solution(mesh):
    return jax.shard_map(
        on_device,
        mesh=mesh,
        in_specs=(
            P("section", "dp", "feat"),
            P("dp", ("section", "feat")),
            P(("section", "feat")),
            P(("section", "feat")),
            P(("section", "feat"), "dp"),
            P(),
            P("dp", ("section", "feat")),
            P("dp", ("section", "feat")),
            P(("section", "feat"), "dp"),
            P(("section", "feat"), "dp"),
        ),
        out_specs=(
            P("dp", ("section", "feat")),
            P("dp", ("section", "feat")),
            P("dp", ("section", "feat")),
            P(("section", "feat"), "dp"),
            P(("section", "feat"), "dp"),
            P(("section", "feat"), "dp"),
        ),
        check_vma=False,
    )
```

profile of v0, /device:TPU:0, one launch (start us, length us, event | category | flops | bytes accessed | tf_op | source)
XLA Modules:
  0.0 630.2 jit_solution(8954610613970382083)
XLA Ops:
  7.2 0.0 all-gather.5.cloned.1.call-start
  7.2 1.4 bitcast_convert_fusion
  8.6 86.1 %all-reduce.1 = bf16[512,1152]{1,0:T(8,128)(2,1)} all-reduce(f32[512,1152]{1,0:T(8,128)S(1)} %bitcast_convert_fusion), channel_id=1, replica_groups=mesh['section'=4,'feat'=4,'dp'=2] {'section'}, use_global_device_ids=true, to_apply=%region_0.0 | all-reduce | flops 589824 | bytes 3538944 | tf_op jit(solution)/shard_map/psum | solution.py:38
  94.8 0.0 all-gather.5.cloned.1.call-update
  94.8 0.0 copy-start.2
  94.8 0.0 all-gather.7.cloned.1.call-start
  94.9 0.7 all-gather.7.cloned.1.call-update
  95.6 0.0 all-gather.9.cloned.1.call-start
  95.6 0.7 all-gather.9.cloned.1.call-update
  96.3 0.0 reduce-scatter.4.cloned.1.call-start
  96.4 0.0 copy-done.2
  96.4 0.0 copy-start
  96.4 87.7 %all-gather.5.cloned.1.call-done = bf16[512,4608]{1,0:T(8,128)(2,1)} async-done(((bf16[512,1152]{1,0:T(8,128)(2,1)}), bf16[512,4608]{1,0:T(8,128)(2,1)}) %all-gather.5.cloned.1.call-update) | async-done | bytes 4718608 | tf_op jit(solution)/shard_map/all_gather | solution.py:39
  184.1 21.6 %all-gather.7.cloned.1.call-done = bf16[4608,1024]{1,0:T(8,128)(2,1)} async-done(((bf16[2304,1024]{1,0:T(8,128)(2,1)}), bf16[4608,1024]{1,0:T(8,128)(2,1)}) %all-gather.7.cloned.1.call-update) | async-done | bytes 9437200 | tf_op jit(solution)/shard_map/all_gather | solution.py:46
  205.7 9.0 %fusion.15 = f32[512,1024]{1,0:T(8,128)S(1)} fusion(bf16[512,4608]{1,0:T(8,128)(2,1)} %all-gather.5.cloned.1.call-done, bf16[4608,1024]{1,0:T(8,128)(2,1)} %all-gather.7.cloned.1.call-done), kind=kOutput, calls=%fused_computation.24 | convolution fusion | flops 4831838208 | bytes 16252928 | tf_op jit(solution)/shard_map/dot_general | solution.py:44
  214.7 15.4 %all-gather.9.cloned.1.call-done = bf16[1024,4608]{1,0:T(8,128)(2,1)} async-done(((bf16[1024,2304]{1,0:T(8,128)(2,1)}), bf16[1024,4608]{1,0:T(8,128)(2,1)}) %all-gather.9.cloned.1.call-update) | async-done | bytes 9437200 | tf_op jit(solution)/shard_map/all_gather | solution.py:54
  230.1 0.0 copy-done
  230.1 11.3 %fusion.11 = f32[512,4608]{1,0:T(8,128)} fusion(bf16[1024,4608]{1,0:T(8,128)(2,1)} %all-gather.9.cloned.1.call-done, f32[512,1024]{1,0:T(8,128)S(1)} %fusion.15, f32[1024]{0:T(1024)S(1)} %add_multiply_fusion.1, f32[1024]{0:T(1024)S(1)} %copy-done), kind=kOutput, calls=%fused_computation.23 | convolution fusion | flops 4836032512 | bytes 20979712 | tf_op jit(solution)/shard_map/dot_general | solution.py:59
  241.3 0.0 copy-start.1
  241.3 0.0 reduce-scatter.4.cloned.1.call-update
  241.4 0.0 all-gather.11.cloned.1.call-start
  241.4 172.9 %reduce-scatter.4.cloned.1.call-done = f32[32,4608]{1,0:T(8,128)} async-done(((f32[512,4608]{1,0:T(8,128)}), f32[32,4608]{1,0:T(8,128)}) %reduce-scatter.4.cloned.1.call-update) | async-done | bytes 589840 | tf_op jit(solution)/shard_map/reduce_scatter | solution.py:58
  414.3 0.0 copy-done.1
  414.3 1.9 multiply_convert_fusion.1
  416.2 0.0 all-gather.11.cloned.1.call-update
  416.3 0.0 reduce-scatter.6.cloned.1.call-start
  416.3 80.0 %all-gather.11.cloned.1.call-done = bf16[512,4608]{1,0:T(8,128)(2,1)} async-done(((bf16[32,4608]{1,0:T(8,128)(2,1)}), bf16[512,4608]{1,0:T(8,128)(2,1)}) %all-gather.11.cloned.1.call-update) | async-done | bytes 4718608 | tf_op jit(solution)/shard_map/all_gather | solution.py:67
  496.3 19.5 %convolution_bitcast_fusion = f32[4608,1024]{0,1:T(8,128)} fusion(bf16[512,4608]{1,0:T(8,128)(2,1)} %all-gather.5.cloned.1.call-done, f32[512,1024]{1,0:T(8,128)S(1)} %fusion.15, bf16[512,4608]{1,0:T(8,128)(2,1)} %all-gather.11.cloned.1.call-done, bf16[1024,4608]{1,0:T(8,128)(2,1)} %all-gather.9.cloned.1.call-done, f32[1024]{0:T(1024)S(1)} %add_multiply_fusion.1, ...), kind=kOutput, calls=%fused_computation.2 | convolution fusion | flops 9670492160 | bytes 39854080 | tf_op jit(solution)/shard_map/dot_general | solution.py:78
  515.9 0.0 reduce-scatter.6.cloned.1.call-update
  515.9 0.2 reduce-scatter.8.cloned.1.call-start
  516.1 16.0 %fusion.9 = f32[1024,4608]{1,0:T(8,128)} fusion(bf16[512,4608]{1,0:T(8,128)(2,1)} %all-gather.11.cloned.1.call-done, f32[512,1024]{1,0:T(8,128)S(1)} %fusion.15, f32[1024]{0:T(1024)S(1)} %add_multiply_fusion.1, f32[1024]{0:T(1024)S(1)} %copy-done), kind=kOutput, calls=%fused_computation.22 | convolution fusion | flops 4836032512 | bytes 25698304 | tf_op jit(solution)/shard_map/dot_general | solution.py:68
  532.2 0.0 reduce-scatter.8.cloned.1.call-update
  532.2 10.7 %copy.16 = f32[2304,1024]{0,1:T(8,128)} copy(f32[2304,1024]{1,0:T(8,128)} %param.16) | data formatting | bytes 18874368 | tf_op args[6]
  542.9 9.7 %copy.17 = f32[2304,1024]{0,1:T(8,128)} copy(f32[2304,1024]{1,0:T(8,128)} %param.17) | data formatting | bytes 18874368 | tf_op args[7]
  552.6 0.0 reduce-scatter.6.cloned.1.call-done
  552.6 25.6 %divide_convert_fusion.1 = (bf16[2304,1024]{0,1:T(8,128)(2,1)}, f32[2304,1024]{0,1:T(8,128)}, f32[2304,1024]{0,1:T(8,128)}) fusion(f32[2304,1024]{0,1:T(8,128)} %reduce-scatter.6.cloned.1.call-done, f32[2304,1024]{0,1:T(8,128)} %copy.16, f32[2304,1024]{0,1:T(8,128)} %copy.17), kind=kLoop, calls=%fused_computation.7 | loop fusion | flops 28311552 | bytes 51904512 | tf_op jit(solution)/shard_map/convert_element_type | solution.py:19
  578.2 6.6 %copy.18 = bf16[2304,1024]{1,0:T(8,128)(2,1)} copy(bf16[2304,1024]{0,1:T(8,128)(2,1)} %get-tuple-element.15) | data formatting | bytes 9437184
  584.8 9.6 %copy.19 = f32[2304,1024]{1,0:T(8,128)} copy(f32[2304,1024]{0,1:T(8,128)} %get-tuple-element.16) | data formatting | bytes 18874368
  594.4 9.6 %copy.20 = f32[2304,1024]{1,0:T(8,128)} copy(f32[2304,1024]{0,1:T(8,128)} %get-tuple-element.17) | data formatting | bytes 18874368
  604.0 0.0 reduce-scatter.8.cloned.1.call-done
  604.0 19.4 %divide_convert_fusion = (bf16[1024,2304]{1,0:T(8,128)(2,1)}, f32[1024,2304]{1,0:T(8,128)}, f32[1024,2304]{1,0:T(8,128)}) fusion(f32[1024,2304]{1,0:T(8,128)} %reduce-scatter.8.cloned.1.call-done, f32[1024,2304]{1,0:T(8,128)} %param.18, f32[1024,2304]{1,0:T(8,128)} %param.19), kind=kLoop, calls=%fused_computation.5 | loop fusion | flops 28311552 | bytes 51904512 | tf_op jit(solution)/shard_map/convert_element_type | solution.py:19
  (1 shorter events, 0.0 us)
Async XLA Ops:
  7.2 176.9 %all-gather.5.cloned.1.call-start = ((), (), s32[]{:S(2)}) async-start(), calls=%async_computation.3 | async-start | bytes 5898240 | tf_op jit(solution)/shard_map/all_gather | solution.py:39
  94.8 1.5 copy-start.2
  94.8 110.9 %all-gather.7.cloned.1.call-start = ((), (), s32[]{:S(2)}) async-start(), calls=%async_computation.4 | async-start | bytes 14155776 | tf_op jit(solution)/shard_map/all_gather | solution.py:46
  95.6 134.5 %all-gather.9.cloned.1.call-start = ((), (), s32[]{:S(2)}) async-start(), calls=%async_computation.5 | async-start | bytes 14155776 | tf_op jit(solution)/shard_map/all_gather | solution.py:54
  96.3 318.0 %reduce-scatter.4.cloned.1.call-start = ((), (), s32[]{:S(2)}) async-start(), calls=%async_computation.6 | async-start | bytes 10027008 | tf_op jit(solution)/shard_map/reduce_scatter | solution.py:58
  96.4 133.7 %copy-start = (f32[1024]{0:T(1024)S(1)}, f32[1024]{0:T(1024)}, u32[]{:S(2)}) copy-start(f32[1024]{0:T(1024)} %param.12) | copy-start | bytes 12292
  241.3 173.0 %copy-start.1 = (f32[4608]{0:T(1024)S(1)}, f32[4608]{0:T(1024)}, u32[]{:S(2)}) copy-start(f32[4608]{0:T(1024)} %param.15) | copy-start | bytes 55300
  241.4 255.0 %all-gather.11.cloned.1.call-start = ((), (), s32[]{:S(2)}) async-start(), calls=%async_computation.7 | async-start | bytes 5013504 | tf_op jit(solution)/shard_map/all_gather | solution.py:67
  416.3 136.4 %reduce-scatter.6.cloned.1.call-start = ((), (), s32[]{:S(2)}) async-start(), calls=%async_computation.8 | async-start | bytes 28311552 | tf_op jit(solution)/shard_map/reduce_scatter | solution.py:77
  515.9 88.1 %reduce-scatter.8.cloned.1.call-start = ((), (), s32[]{:S(2)}) async-start(), calls=%async_computation.9 | async-start | bytes 28311552 | tf_op jit(solution)/shard_map/reduce_scatter | solution.py:71
Sparse Core Ops, SparseCore 0:
  94.9 89.0 all-gather.4
  185.6 20.0 all-gather.6
  207.3 22.7 all-gather.8
  241.5 172.7 reduce-scatter.3
  417.5 78.8 all-gather.10
  516.0 25.1 reduce-scatter.5
  543.5 27.7 reduce-scatter.7
where the time goes:
time: 631 us; the launch traced here: 630 us
  waiting for transfers between devices  379 us (60%)
  blocking collectives  86.1 us (14%)
  matrix products  55.8 us (9%)
  other arithmetic  48.4 us (8%)
  local copies, waits for them, and re-layouts  46.2 us (7%)
  between operations  14.2 us (2%)
    reduce_scatter x1, waiting for transfers between devices, on_device(): lax.psum_scatter(jnp.dot(codes, dec_full, preferred_element_type=jnp.floa...  173 us
    all_gather x1, waiting for transfers between devices, on_device(): resid = lax.all_gather(summed, 'feat', axis=1, tiled=True)  87.7 us
    psum x1, blocking collectives, on_device(): summed = lax.psum(own_part, 'section').astype(jnp.bfloat16)  86.1 us
    all_gather x1, waiting for transfers between devices, on_device(): lax.all_gather(error_part, ('section', 'feat'), axis=0, tiled=True)  80 us
    unnamed x11, local copies, waits for them, and re-layouts  46.2 us
    convert_element_type x2, other arithmetic, adam_moves(): (moment_new / fix_first / (jnp.sqrt(second_new / fix_second) + epsilon))....  45 us
    all_gather x1, waiting for transfers between devices, on_device(): lax.all_gather(enc_weight, 'dp', axis=0, tiled=True)  21.6 us
    dot_general x1, matrix products, on_device(): lax.dot_general(columns, pre_grad, (((0,), (0,)), ((), ())), preferred_el...  19.5 us
  transfers between devices with their start and end apart: 7, of which 5 were waited for; matrix products, arithmetic and copies ran while one was open for 15% of the time, Pallas kernels for 0%

commit v1 on v0

--- a/solution.py
+++ b/solution.py
@@ -36,7 +36,17 @@
 ):
     own_part = section_outputs[0].astype(jnp.float32)
     summed = lax.psum(own_part, "section").astype(jnp.bfloat16)
-    resid = lax.all_gather(summed, "feat", axis=1, tiled=True)
+    local_part = lax.axis_size("feat")
+    passed = lax.axis_index("feat")
+    high, tile_out, b_next = (local_part, passed, summed.shape[1])
+    big, y2 = (summed, 1)
+    while y2 < high:
+        big = jnp.concatenate(
+            [big, lax.ppermute(big, "feat", tuple(((kk, (kk - y2) % high) for kk in range(high))))],
+            1,
+        )
+        y2 = 2 * y2
+    resid = jnp.roll(big, tile_out * b_next, 1)
     tok_rows = resid.shape[0]
     token_total = tok_rows * lax.axis_size("dp")
     columns = resid

time: 631 us -> 602 us (0.954)
  local copies, waits for them, and re-layouts: 46.2 us -> 10.9 us
    ppermute x0 -> x2, waiting for transfers between devices: none -> 122 us  [on_device(): lax.ppermute(big, 'feat', tuple(((kk, (kk - y2) % high) for kk in range(h...]
    all_gather x1 -> x0, waiting for transfers between devices: 87.7 us -> none  [on_device(): resid = lax.all_gather(summed, 'feat', axis=1, tiled=True)]
    unnamed x11 -> x13, local copies, waits for them, and re-layouts: 46.2 us -> 7.65 us
    all_gather x1, waiting for transfers between devices: 21.6 us -> 0.01 us  [on_device(): lax.all_gather(enc_weight, 'dp', axis=0, tiled=True)]
    all_gather x1, waiting for transfers between devices: 15.4 us -> 0.02 us  [on_device(): dec_full = lax.all_gather(dec_weight, 'dp', axis=1, tiled=True)]
    reduce_scatter x1, waiting for transfers between devices: 0.01 us -> 7.63 us  [on_device(): lax.psum_scatter(lax.dot_general(columns, pre_grad, (((0,), (0,)), ((), (...]
  transfers between devices with their start and end apart: 7 -> 8, of which waited for: 5 -> 6; matrix products, arithmetic and copies ran while one was open for 15% -> 11% of each run, Pallas kernels for 0% -> 0%
where the time goes in v1:
time: 602 us; the launch traced here: 601 us
  waiting for transfers between devices  384 us (64%)
  blocking collectives  85.7 us (14%)
  matrix products  55.2 us (9%)
  other arithmetic  46.4 us (8%)
  between operations  14.2 us (2%)
  local copies, waits for them, and re-layouts  10.9 us (2%)
    reduce_scatter x1, waiting for transfers between devices, on_device(): lax.psum_scatter(jnp.dot(codes, dec_full, preferred_element_type=jnp.floa...  171 us
    ppermute x2, waiting for transfers between devices, on_device(): lax.ppermute(big, 'feat', tuple(((kk, (kk - y2) % high) for kk in range(h...  122 us
    psum x1, blocking collectives, on_device(): summed = lax.psum(own_part, 'section').astype(jnp.bfloat16)  85.7 us
    all_gather x1, waiting for transfers between devices, on_device(): lax.all_gather(error_part, ('section', 'feat'), axis=0, tiled=True)  79.9 us
    convert_element_type x2, other arithmetic, adam_moves(): (moment_new / fix_first / (jnp.sqrt(second_new / fix_second) + epsilon))....  42.6 us
    dot_general x1, matrix products, on_device(): lax.dot_general(columns, pre_grad, (((0,), (0,)), ((), ())), preferred_el...  23.3 us
  transfers between devices with their start and end apart: 8, of which 6 were waited for; matrix products, arithmetic and copies ran while one was open for 11% of the time, Pallas kernels for 0%

profile of v1, /device:TPU:0, one launch (start us, length us, event | category | flops | bytes accessed | tf_op | source)
XLA Modules:
  0.0 601.4 jit_solution(13412692581620972966)
XLA Ops:
  7.2 0.0 copy-start
  7.2 0.0 all-gather.4.cloned.1.call-start
  7.2 0.7 all-gather.4.cloned.1.call-update
  7.9 0.0 copy-start.3
  7.9 0.0 all-gather.6.cloned.1.call-start
  8.0 0.7 all-gather.6.cloned.1.call-update
  8.7 0.0 reduce-scatter.4.cloned.1.call-start
  8.7 0.0 copy-done
  8.7 0.2 bitcast_convert_fusion
  8.9 85.7 %all-reduce.1 = bf16[512,1152]{1,0:T(8,128)(2,1)S(1)} all-reduce(f32[512,1152]{1,0:T(8,128)S(1)} %bitcast_convert_fusion), channel_id=1, replica_groups=mesh['section'=4,'feat'=4,'dp'=2] {'section'}, use_global_device_ids=true, to_apply=%region_0.0 | all-reduce | flops 589824 | bytes 3538944 | tf_op jit(solution)/shard_map/psum | solution.py:38
  94.6 3.7 collective-permute-start
  98.3 23.4 %collective-permute-done = bf16[512,1152]{1,0:T(8,128)(2,1)S(1)} collective-permute-done((bf16[512,1152]{1,0:T(8,128)(2,1)S(1)}, bf16[512,1152]{1,0:T(8,128)(2,1)S(1)}, u32[]{:S(2)}, u32[]{:S(2)}) %collective-permute-start) | collective-permute-done | bytes 1179680 | tf_op jit(solution)/shard_map/ppermute | solution.py:45
  121.7 1.6 pad_maximum_fusion
  123.3 1.5 collective-permute-start.1
  124.7 0.0 copy-done.3
  124.7 1.1 constant_dynamic-update-slice_fusion.5
  125.8 1.1 constant_dynamic-update-slice_fusion.4
  126.9 98.4 %collective-permute-done.1 = bf16[512,2304]{1,0:T(8,128)(2,1)} collective-permute-done((bf16[512,2304]{1,0:T(8,128)(2,1)}, bf16[512,2304]{1,0:T(8,128)(2,1)}, u32[]{:S(2)}, u32[]{:S(2)}) %collective-permute-start.1) | collective-permute-done | bytes 2359328 | tf_op jit(solution)/shard_map/ppermute | solution.py:45
  225.4 3.2 constant_dynamic-update-slice_fusion.3
  228.6 1.1 constant_dynamic-update-slice_fusion.2
  229.7 1.1 constant_dynamic-update-slice_fusion.1
  230.8 3.2 constant_dynamic-update-slice_fusion
  234.0 0.0 copy-start.1
  234.0 0.0 all-gather.4.cloned.1.call-done
  234.0 9.1 %fusion.4 = f32[512,1024]{1,0:T(8,128)S(1)} fusion(bf16[4608,1024]{1,0:T(8,128)(2,1)} %all-gather.4.cloned.1.call-done, bf16[512,9216]{1,0:T(8,128)(2,1)} %constant_dynamic-update-slice_fusion, s32[]{:T(128)S(6)} %select_n.21), kind=kOutput, calls=%fused_computation.10 | convolution fusion | flops 4831838208 | bytes 16252932 | tf_op jit(solution)/shard_map/dot_general | solution.py:54
  243.2 0.0 all-gather.6.cloned.1.call-done
  243.2 0.0 copy-done.1
  243.2 11.2 %fusion.13 = f32[512,4608]{1,0:T(8,128)} fusion(bf16[1024,4608]{1,0:T(8,128)(2,1)} %all-gather.6.cloned.1.call-done, f32[512,1024]{1,0:T(8,128)S(1)} %fusion.4, f32[1024]{0:T(1024)S(1)} %add_multiply_fusion.1, f32[1024]{0:T(1024)S(1)} %copy-done.1), kind=kOutput, calls=%fused_computation.31 | convolution fusion | flops 4836032512 | bytes 20979712 | tf_op jit(solution)/shard_map/dot_general | solution.py:69
  254.4 0.0 copy-start.2
  254.4 0.0 reduce-scatter.4.cloned.1.call-update
  254.5 0.0 all-gather.8.cloned.1.call-start
  254.5 170.9 %reduce-scatter.4.cloned.1.call-done = f32[32,4608]{1,0:T(8,128)} async-done(((f32[512,4608]{1,0:T(8,128)}), f32[32,4608]{1,0:T(8,128)}) %reduce-scatter.4.cloned.1.call-update) | async-done | bytes 589840 | tf_op jit(solution)/shard_map/reduce_scatter | solution.py:68
  425.4 0.0 copy-done.2
  425.4 2.1 multiply_convert_fusion.1
  427.5 0.0 all-gather.8.cloned.1.call-update
  427.5 0.0 reduce-scatter.8.cloned.1.call-start
  427.6 79.9 %all-gather.8.cloned.1.call-done = bf16[512,4608]{1,0:T(8,128)(2,1)} async-done(((bf16[32,4608]{1,0:T(8,128)(2,1)}), bf16[512,4608]{1,0:T(8,128)(2,1)}) %all-gather.8.cloned.1.call-update) | async-done | bytes 4718608 | tf_op jit(solution)/shard_map/all_gather | solution.py:77
  507.5 11.5 %fusion.11 = f32[1024,4608]{1,0:T(8,128)} fusion(bf16[512,4608]{1,0:T(8,128)(2,1)} %all-gather.8.cloned.1.call-done, f32[512,1024]{1,0:T(8,128)S(1)} %fusion.4, f32[1024]{0:T(1024)S(1)} %add_multiply_fusion.1, f32[1024]{0:T(1024)S(1)} %copy-done.1), kind=kOutput, calls=%fused_computation.30 | convolution fusion | flops 4836032512 | bytes 25698304 | tf_op jit(solution)/shard_map/dot_general | solution.py:78
  519.0 0.0 reduce-scatter.8.cloned.1.call-update
  519.0 0.2 reduce-scatter.6.cloned.1.call-start
  519.3 23.3 %fusion.2 = f32[4608,1024]{1,0:T(8,128)} fusion(bf16[512,9216]{1,0:T(8,128)(2,1)} %constant_dynamic-update-slice_fusion, s32[]{:T(128)S(6)} %select_n.21, f32[512,1024]{1,0:T(8,128)S(1)} %fusion.4, bf16[512,4608]{1,0:T(8,128)(2,1)} %all-gather.8.cloned.1.call-done, bf16[1024,4608]{1,0:T(8,128)(2,1)} %all-gather.6.cloned.1.call-done, ...), kind=kOutput, calls=%fused_computation.8 | convolution fusion | flops 9670492160 | bytes 39854084 | tf_op jit(solution)/shard_map/dot_general | solution.py:88
  542.5 0.0 reduce-scatter.6.cloned.1.call-update
  542.6 1.8 reduce-scatter.8.cloned.1.call-done
  544.3 22.4 %divide_convert_fusion = (bf16[1024,2304]{1,0:T(8,128)(2,1)}, f32[1024,2304]{1,0:T(8,128)}, f32[1024,2304]{1,0:T(8,128)}) fusion(f32[1024,2304]{1,0:T(8,128)} %reduce-scatter.8.cloned.1.call-done, f32[1024,2304]{1,0:T(8,128)} %param.18, f32[1024,2304]{1,0:T(8,128)} %param.19), kind=kLoop, calls=%fused_computation.4 | loop fusion | flops 28311552 | bytes 51904512 | tf_op jit(solution)/shard_map/convert_element_type | solution.py:19
  566.7 7.6 %reduce-scatter.6.cloned.1.call-done = f32[2304,1024]{1,0:T(8,128)} async-done(((f32[4608,1024]{1,0:T(8,128)}), f32[2304,1024]{1,0:T(8,128)}) %reduce-scatter.6.cloned.1.call-update) | async-done | bytes 9437200 | tf_op jit(solution)/shard_map/reduce_scatter | solution.py:87
  574.4 20.1 %divide_convert_fusion.1 = (bf16[2304,1024]{1,0:T(8,128)(2,1)}, f32[2304,1024]{1,0:T(8,128)}, f32[2304,1024]{1,0:T(8,128)}) fusion(f32[2304,1024]{1,0:T(8,128)} %reduce-scatter.6.cloned.1.call-done, f32[2304,1024]{1,0:T(8,128)} %param.16, f32[2304,1024]{1,0:T(8,128)} %param.17), kind=kLoop, calls=%fused_computation.6 | loop fusion | flops 28311552 | bytes 51904512 | tf_op jit(solution)/shard_map/convert_element_type | solution.py:19
  (1 shorter events, 0.0 us)
Async XLA Ops:
  7.2 1.6 copy-start
  7.2 226.9 %all-gather.4.cloned.1.call-start = ((), (), s32[]{:S(2)}) async-start(), calls=%async_computation.3 | async-start | bytes 14155776 | tf_op jit(solution)/shard_map/all_gather | solution.py:56
  7.9 116.8 %copy-start.3 = (s32[1024]{0:T(1024)S(1)}, s32[1024]{0:T(1024)}, u32[]{:S(2)}) copy-start(s32[1024]{0:T(1024)} %param.13) | copy-start | bytes 12292
  7.9 235.3 %all-gather.6.cloned.1.call-start = ((), (), s32[]{:S(2)}) async-start(), calls=%async_computation.4 | async-start | bytes 14155776 | tf_op jit(solution)/shard_map/all_gather | solution.py:64
  8.7 416.8 %reduce-scatter.4.cloned.1.call-start = ((), (), s32[]{:S(2)}) async-start(), calls=%async_computation.5 | async-start | bytes 10027008 | tf_op jit(solution)/shard_map/reduce_scatter | solution.py:68
  94.6 27.1 %collective-permute-start = (bf16[512,1152]{1,0:T(8,128)(2,1)S(1)}, bf16[512,1152]{1,0:T(8,128)(2,1)S(1)}, u32[]{:S(2)}, u32[]{:S(2)}) collective-permute-start(bf16[512,1152]{1,0:T(8,128)(2,1)S(1)} %all-reduce.1), channel_id=1, source_target_pairs={{0,6},{2,0},{4,2},{6,4},{1,7},{3,1},{5,3},{7,5},{8,14},{10,8},{12,... | collective-permute-start | bytes 3538952 | tf_op jit(solution)/shard_map/ppermute | solution.py:45
  123.3 102.1 %collective-permute-start.1 = (bf16[512,2304]{1,0:T(8,128)(2,1)}, bf16[512,2304]{1,0:T(8,128)(2,1)}, u32[]{:S(2)}, u32[]{:S(2)}) collective-permute-start(bf16[512,2304]{1,0:T(8,128)(2,1)} %pad_maximum_fusion), channel_id=1, source_target_pairs={{0,4},{2,6},{4,0},{6,2},{1,5},{3,7},{5,1},{7,3},{8,12},{10,14},{12... | collective-permute-start | bytes 7077896 | tf_op jit(solution)/shard_map/ppermute | solution.py:45
  234.0 9.2 %copy-start.1 = (f32[1024]{0:T(1024)S(1)}, f32[1024]{0:T(1024)}, u32[]{:S(2)}) copy-start(f32[1024]{0:T(1024)} %param.12) | copy-start | bytes 12292
  254.4 171.0 %copy-start.2 = (f32[4608]{0:T(1024)S(1)}, f32[4608]{0:T(1024)}, u32[]{:S(2)}) copy-start(f32[4608]{0:T(1024)} %param.15) | copy-start | bytes 55300
  254.5 253.0 %all-gather.8.cloned.1.call-start = ((), (), s32[]{:S(2)}) async-start(), calls=%async_computation.6 | async-start | bytes 5013504 | tf_op jit(solution)/shard_map/all_gather | solution.py:77
  427.5 116.8 %reduce-scatter.8.cloned.1.call-start = ((), (), s32[]{:S(2)}) async-start(), calls=%async_computation.8 | async-start | bytes 28311552 | tf_op jit(solution)/shard_map/reduce_scatter | solution.py:81
  519.0 55.3 %reduce-scatter.6.cloned.1.call-start = ((), (), s32[]{:S(2)}) async-start(), calls=%async_computation.7 | async-start | bytes 28311552 | tf_op jit(solution)/shard_map/reduce_scatter | solution.py:87
Sparse Core Ops, SparseCore 0:
  9.5 24.3 all-gather.3
  35.5 22.7 all-gather.5
  254.6 170.7 reduce-scatter.3
  428.6 78.8 all-gather.7
  519.1 25.1 reduce-scatter.7
  546.5 27.8 reduce-scatter.5
